TPU v7x, 32 devices: a whole 2x2x4 slice. The times are simulated.
32 devices in a mesh: fsdp: 8 (over y, x, core), ctx: 4 (over z).
Axes of the slice: x: 2, y: 2, z: 4, core: 2. Of those that a mesh axis runs over, the one named last changes fastest.
Arguments:
- tokens: bfloat16 [4096, 8192], P('fsdp'), may hold values from -12 to 12
- wq: bfloat16 [8192, 4096], P('fsdp', 'ctx'), may hold values from -0.0625 to 0.0625
- wo: bfloat16 [4096, 8192], P('ctx', 'fsdp'), may hold values from -1.5 to 1.5
- key_cache: bfloat16 [8192, 1024], P(('fsdp', 'ctx')), may hold values from -500 to 500, as said below
- value_cache: bfloat16 [8192, 1024], P(('fsdp', 'ctx')), may hold values from -6 to 6
- key_blocks: int32 [8, 4, 8], P('fsdp'), may hold values from 0 to 7, as said below
Outputs:
- mixed: bfloat16 [4096, 8192], P('fsdp', 'ctx')
Inputs may be any that keep to these rules, and one draw needn't show every extreme that they name: `key_cache`: keys of order one; a sequence's first block may hold much larger ones. `key_blocks`: for query block b of sequence s, entries 0 to 2 name key blocks 8 - 4 + b - 2, 4 + b - 1 and 4 + b; entries 3 and 4 name blocks 0 and 1; the last 3 entries are random blocks. Counting the random entries of a sequence over its query blocks in order as t = 0, 1, ..., the t-th lies in blocks k * 2 to (k+1) * 2 - 1 with k = 1 + t mod (2); entries may repeat.
All inputs are finite; a program needn't handle non-finite values.
Results may differ from a plain program's by a relative error of at most 0.018.
Values may be sent and summed in bfloat16 or wider, within the bound.
A program may use at most 128 MiB of HBM per device.

v0:
```python
import jax
import jax.numpy as jnp
from jax import lax
from jax.sharding import PartitionSpec as P

HEAD = 128
BLOCK = 128


rope_base = 1000000.0


def rotate(vectors, positions):
    half_width = vectors.shape[-1] // 2
    frequency = rope_base ** (
        -(jnp.arange(half_width, dtype=jnp.float32) * 2.0) / vectors.shape[-1]
    )
    angles = positions.astype(jnp.float32)[:, None] * frequency[None, :]
    cosine_table = jnp.cos(angles)[:, None, :]
    sine_table = jnp.sin(angles)[:, None, :]
    front_half = vectors[..., :half_width]
    back_half = vectors[..., half_width:]
    return jnp.concatenate(
        [
            front_half * cosine_table - back_half * sine_table,
            back_half * cosine_table + front_half * sine_table,
        ],
        axis=-1,
    )


def body(tokens, wq, wo, key_cache, value_cache, key_blocks):
    ctx_count = lax.axis_size("ctx")
    row_count = tokens.shape[0]
    query_cols = wq.shape[1]
    projected = jnp.dot(
        tokens, lax.all_gather(wq, "fsdp", axis=0, tiled=True), preferred_element_type=jnp.float32
    )
    cache_count = key_cache.shape[0]
    key_total = cache_count * ctx_count
    positions = key_total - row_count + jnp.arange(row_count, dtype=jnp.int32)
    query = (
        rotate(projected.reshape(row_count, query_cols // HEAD, HEAD), positions) * HEAD ** (-0.5)
    ).astype(jnp.bfloat16)
    kv_cols = key_cache.shape[1] // ctx_count
    keys_split = key_cache.reshape(cache_count, ctx_count, kv_cols)
    values_split = value_cache.reshape(cache_count, ctx_count, kv_cols)
    keys_moved, values_moved = (
        lax.all_to_all(keys_split, "ctx", split_axis=1, concat_axis=0, tiled=True),
        lax.all_to_all(values_split, "ctx", split_axis=1, concat_axis=0, tiled=True),
    )
    keys_all = keys_moved.reshape(key_total, kv_cols)
    values_all = values_moved.reshape(key_total, kv_cols)
    kv_local = kv_cols // HEAD
    group_size = query_cols // kv_cols
    block_count = key_total // BLOCK
    query_blocks = row_count // BLOCK
    lists = key_blocks[0]
    picked_keys = jnp.take(keys_all.reshape(block_count, BLOCK, kv_local, HEAD), lists, axis=0)
    picked_values = jnp.take(values_all.reshape(block_count, BLOCK, kv_local, HEAD), lists, axis=0)
    shaped = query.reshape(query_blocks, BLOCK, kv_local, group_size, HEAD)
    scores = jnp.einsum(
        "bqkgd,bnskd->bkgqns", shaped, picked_keys, preferred_element_type=jnp.float32
    )
    own_block = block_count - query_blocks + jnp.arange(query_blocks, dtype=jnp.int32)
    own = lists == own_block[:, None]
    causal = jnp.arange(BLOCK)[None, :] <= jnp.arange(BLOCK)[:, None]
    allowed = jnp.logical_or(
        jnp.logical_not(own)[:, None, None, None, :, None], causal[None, None, None, :, None, :]
    )
    scores = jnp.where(allowed, scores, -jnp.inf)
    top_score = jnp.max(scores, axis=(4, 5), keepdims=True)
    raised = jnp.exp(scores - top_score)
    weights = (raised / jnp.sum(raised, axis=(4, 5), keepdims=True)).astype(jnp.bfloat16)
    context = jnp.einsum(
        "bkgqns,bnskd->bqkgd", weights, picked_values, preferred_element_type=jnp.float32
    )
    context = context.astype(jnp.bfloat16).reshape(row_count, query_cols)
    share_terms = jnp.dot(
        context, lax.all_gather(wo, "fsdp", axis=1, tiled=True), preferred_element_type=jnp.float32
    )
    return lax.psum_scatter(
        share_terms.astype(jnp.bfloat16), "ctx", scatter_dimension=1, tiled=True
    )


def solution(mesh):
    in_specs = (
        P("fsdp", None),
        P("fsdp", "ctx"),
        P("ctx", "fsdp"),
        P(("fsdp", "ctx"), None),
        P(("fsdp", "ctx"), None),
        P("fsdp", None, None),
    )
    out_specs = P("fsdp", "ctx")
    return jax.shard_map(body, mesh=mesh, in_specs=in_specs, out_specs=out_specs, check_vma=False)
```

profile of v0, /device:TPU:29, one launch (start us, length us, event | category | flops | bytes accessed | tf_op | source)
XLA Modules:
  0.0 359.2 jit_solution(7544698993434867624)
XLA Ops:
  8.9 4.5 %all-to-all-start = ((bf16[256,4,256]{2,0,1:T(8,128)(2,1)}), bf16[256,4,256]{2,0,1:T(8,128)(2,1)S(1)}, u32[]{:S(2)}, u32[]{:S(2)}) async-start(bf16[256,4,256]{2,0,1:T(8,128)(2,1)} %bitcast.69), calls=%async_computation | async-start | bytes 1048576 | tf_op jit(solution)/shard_map/all_to_all | solution.py:50
  14.4 10.3 %all-to-all-done = bf16[256,4,256]{2,0,1:T(8,128)(2,1)S(1)} async-done(((bf16[256,4,256]{2,0,1:T(8,128)(2,1)}), bf16[256,4,256]{2,0,1:T(8,128)(2,1)S(1)}, u32[]{:S(2)}, u32[]{:S(2)}) %all-to-all-start) | async-done | bytes 524320 | tf_op jit(solution)/shard_map/all_to_all | solution.py:50
  24.7 6.8 %all-to-all-start.1 = ((bf16[256,4,256]{2,0,1:T(8,128)(2,1)}), bf16[256,4,256]{2,0,1:T(8,128)(2,1)}, u32[]{:S(2)}, u32[]{:S(2)}) async-start(bf16[256,4,256]{2,0,1:T(8,128)(2,1)} %bitcast.68), calls=%async_computation.1 | async-start | bytes 1048576 | tf_op jit(solution)/shard_map/all_to_all | solution.py:49
  32.6 5.4 %gather_fusion = bf16[32,128,2,128]{3,2,1,0:T(2,128)(2,1)S(1)} fusion(bf16[8,128,2,128]{3,2,1,0:T(2,128)(2,1)S(1)} %reshape_reshape.6, s32[1024]{0:T(1024)S(1)} %pad_clamp_fusion), kind=kCustom, calls=%fused_computation.clone | custom fusion | bytes 4194432 | tf_op jit(solution)/shard_map/jit(_take)/gather | solution.py:60
  38.0 1.9 copy.9
  39.9 3.0 all-to-all-done.1
  42.9 1.2 reshape_reshape.7
  44.1 5.4 %gather_fusion.1 = bf16[32,128,2,128]{3,2,1,0:T(2,128)(2,1)S(1)} fusion(bf16[8,128,2,128]{3,2,1,0:T(2,128)(2,1)S(1)} %reshape_reshape.7, s32[1024]{0:T(1024)S(1)} %pad_clamp_fusion), kind=kCustom, calls=%fused_computation.1.clone | custom fusion | bytes 4194432 | tf_op jit(solution)/shard_map/jit(_take)/gather | solution.py:59
  50.0 1.0 copy-done
  51.1 3.2 select_bitcast_fusion.1
  54.3 45.3 %all-gather.3.cloned.1.call-done = bf16[8192,1024]{1,0:T(8,128)(2,1)} async-done(((bf16[1024,1024]{1,0:T(8,128)(2,1)}), bf16[8192,1024]{1,0:T(8,128)(2,1)}) %all-gather.3.cloned.1.call-update) | async-done | bytes 16777232 | tf_op jit(solution)/shard_map/all_gather | solution.py:37
  99.6 15.2 %fusion.23 = f32[512,1024]{0,1:T(8,128)} fusion(bf16[512,8192]{1,0:T(8,128)(2,1)} %param.8, bf16[8192,1024]{1,0:T(8,128)(2,1)} %all-gather.3.cloned.1.call-done), kind=kOutput, calls=%fused_computation.39 | convolution fusion | flops 8589934592 | bytes 27262976 | tf_op jit(solution)/shard_map/reshape | solution.py:43
  114.8 2.9 multiply_subtract_fusion
  117.7 1.3 concatenate.8
  119.0 1.7 copy.14
  120.8 2.6 concatenate.9
  123.3 2.8 copy.15
  126.1 10.4 %fusion = (f32[4,2,4,128]{3,2,1,0:T(4,128)S(1)}, f32[4,2,8,128,128,4]{4,3,5,2,1,0:T(8,128)}) fusion(pred[4,128,8,128]{1,3,2,0:T(8,128)(4,1)S(1)} %broadcast_or_fusion, f32[4,128,2,4,64]{4,1,3,2,0:T(8,128)} %copy.15, f32[4,128,2,4,64]{4,1,3,2,0:T(8,128)S(1)} %copy.14, bf16[4,8,128,2,128,1]{4,2,3,1,0,5:T(8,128)(2,1)} %get-tuple-element.13), kind=kOutput, calls=%fused_computation.5 | convolution fusion | flops 1083699200 | bytes 21512192 | tf_op jit(solution)/shard_map/bqkgd,bnskd->bkgqns/dot_general | solution.py:62
  136.6 9.0 %fusion.1 = f32[4,2,4,128]{3,2,1,0:T(4,128)S(1)} fusion(f32[4,2,8,128,128,4]{4,3,5,2,1,0:T(8,128)} %get-tuple-element.15, f32[4,2,4,128]{3,2,1,0:T(4,128)S(1)} %get-tuple-element.14, pred[4,128,8,128]{1,3,2,0:T(8,128)(4,1)S(1)} %broadcast_or_fusion), kind=kLoop, calls=%fused_computation.6 | loop fusion | flops 12578816 | bytes 17334272 | tf_op jit(solution)/shard_map/reduce_sum | solution.py:74
  145.6 9.0 %fusion.12 = bf16[4,128,2,4,128]{1,4,3,2,0:T(8,128)(2,1)} fusion(bf16[4,8,128,2,128,1]{4,2,3,1,0,5:T(8,128)(2,1)S(1)} %copy-done.1, f32[4,2,8,128,128,4]{4,3,5,2,1,0:T(8,128)} %get-tuple-element.15, f32[4,2,4,128]{3,2,1,0:T(4,128)S(1)} %fusion.1, f32[4,2,4,128]{3,2,1,0:T(4,128)S(1)} %get-tuple-element.14, pred[4,128,8,128]{1,3,2,0:T(8,128)(4,1)S(1)} %broadcast_or_fusion), kind=kOutput, calls=%fused_computation.18 | convolution fusion | flops 1091043328 | bytes 20480000 | tf_op jit(solution)/shard_map/bkgqns,bnskd->bqkgd/dot_general | solution.py:75
  154.6 1.8 copy.19
  157.2 34.1 %all-gather.5.cloned.1.call-done = bf16[1024,8192]{1,0:T(8,128)(2,1)} async-done(((bf16[1024,1024]{1,0:T(8,128)(2,1)}), bf16[1024,8192]{1,0:T(8,128)(2,1)}) %all-gather.5.cloned.1.call-update) | async-done | bytes 16777232 | tf_op jit(solution)/shard_map/all_gather | solution.py:80
  191.3 16.8 %convolution_convert_fusion = bf16[512,8192]{1,0:T(8,128)(2,1)} fusion(bf16[512,1024]{1,0:T(8,128)(2,1)S(1)} %reshape.128, bf16[1024,8192]{1,0:T(8,128)(2,1)} %all-gather.5.cloned.1.call-done), kind=kOutput, calls=%fused_computation.7 | convolution fusion | flops 8594128896 | bytes 26214400 | tf_op jit(solution)/shard_map/dot_general | solution.py:79
  208.1 144.6 %reduce-scatter.2.cloned.1.call-done = bf16[512,2048]{1,0:T(8,128)(2,1)} async-done(((bf16[512,8192]{1,0:T(8,128)(2,1)}), bf16[512,2048]{1,0:T(8,128)(2,1)}) %reduce-scatter.2.cloned.1.call-update) | async-done | bytes 2097168 | tf_op jit(solution)/shard_map/reduce_scatter | solution.py:82
  (30 shorter events, 5.6 us)
Async XLA Ops:
  6.5 1.5 copy-start.2
  6.5 93.1 %all-gather.3.cloned.1.call-start = ((), (), s32[]{:S(2)}) async-start(), calls=%async_computation.3 | async-start | bytes 18874368 | tf_op jit(solution)/shard_map/all_gather | solution.py:37
  7.3 6.1 %copy-start.4 = (s32[1,4,8]{2,1,0:T(4,128)S(1)}, s32[1,4,8]{2,1,0:T(4,128)}, u32[]{:S(2)}) copy-start(s32[1,4,8]{2,1,0:T(4,128)} %param.13) | copy-start | bytes 388
  7.3 6.2 %copy-start.3 = (bf16[256,1024]{1,0:T(8,128)(2,1)S(1)}, bf16[256,1024]{1,0:T(8,128)(2,1)}, u32[]{:S(2)}) copy-start(bf16[256,1024]{1,0:T(8,128)(2,1)} %param.11) | copy-start | bytes 1572868
  7.3 184.0 %all-gather.5.cloned.1.call-start = ((), (), s32[]{:S(2)}) async-start(), calls=%async_computation.4 | async-start | bytes 18874368 | tf_op jit(solution)/shard_map/all_gather | solution.py:80
  8.9 15.9 %all-to-all-start = ((bf16[256,4,256]{2,0,1:T(8,128)(2,1)}), bf16[256,4,256]{2,0,1:T(8,128)(2,1)S(1)}, u32[]{:S(2)}, u32[]{:S(2)}) async-start(bf16[256,4,256]{2,0,1:T(8,128)(2,1)} %bitcast.69), calls=%async_computation | async-start | bytes 1048576 | tf_op jit(solution)/shard_map/all_to_all | solution.py:50
  24.7 18.2 %all-to-all-start.1 = ((bf16[256,4,256]{2,0,1:T(8,128)(2,1)}), bf16[256,4,256]{2,0,1:T(8,128)(2,1)}, u32[]{:S(2)}, u32[]{:S(2)}) async-start(bf16[256,4,256]{2,0,1:T(8,128)(2,1)} %bitcast.68), calls=%async_computation.1 | async-start | bytes 1048576 | tf_op jit(solution)/shard_map/all_to_all | solution.py:49
  31.5 321.1 %reduce-scatter.2.cloned.1.call-start = ((), (), s32[]{:S(2)}) async-start(), calls=%async_computation.5 | async-start | bytes 10485760 | tf_op jit(solution)/shard_map/reduce_scatter | solution.py:82
  49.5 1.6 copy-start
  136.6 9.0 %copy-start.1 = (bf16[4,8,128,2,128,1]{4,2,3,1,0,5:T(8,128)(2,1)S(1)}, bf16[4,8,128,2,128,1]{4,2,3,1,0,5:T(8,128)(2,1)}, u32[]{:S(2)}) copy-start(bf16[4,8,128,2,128,1]{4,2,3,1,0,5:T(8,128)(2,1)} %get-tuple-element.12) | copy-start | bytes 6291460
Sparse Core Ops, SparseCore 0:
  9.2 90.3 all-gather.2
  101.5 89.7 all-gather.4
  208.2 144.4 reduce-scatter.1
where the time goes:
time: 362 us; the launch traced here: 359 us
  waiting for transfers between devices  239 us (66%)
  matrix products  51.4 us (14%)
  local copies, waits for them, and re-layouts  28.3 us (8%)
  other arithmetic  16.1 us (4%)
  between operations  13.2 us (4%)
  starting transfers between devices  11.4 us (3%)
    reduce_scatter x1, waiting for transfers between devices, body(): lax.psum_scatter(share_terms.astype(jnp.bfloat16), 'ctx', scatter_dimensi...  145 us
    all_gather x1, waiting for transfers between devices, body(): lax.all_gather(wq, 'fsdp', axis=0, tiled=True)  45.3 us
    all_gather x1, waiting for transfers between devices, body(): lax.all_gather(wo, 'fsdp', axis=1, tiled=True)  34.1 us
    dot_general x1, matrix products, body(): jnp.dot(context, lax.all_gather(wo, 'fsdp', axis=1, tiled=True), preferre...  16.8 us
    reshape x1, matrix products, body(): projected.reshape(row_count, query_cols // HEAD, HEAD)  15.2 us
    dot_general x1, matrix products, body(): jnp.einsum('bqkgd,bnskd->bkgqns', shaped, picked_keys, preferred_element_...  10.4 us
    all_to_all x1, waiting for transfers between devices, body(): lax.all_to_all(values_split, 'ctx', split_axis=1, concat_axis=0, tiled=True)  10.3 us
    dot_general x1, matrix products, body(): jnp.einsum('bkgqns,bnskd->bqkgd', weights, picked_values, preferred_eleme...  9.03 us
  transfers between devices with their start and end apart: 5, of which 5 were waited for; matrix products, arithmetic and copies ran while one was open for 22% of the time, Pallas kernels for 0%

commit v1 on v0

v1 whole, which is shorter than its diff:
```python
import functools

import jax
import jax.numpy as jnp
from jax import lax
from jax.experimental import pallas as pl
from jax.experimental.pallas import tpu as pltpu
from jax.sharding import PartitionSpec as P

HEAD = 128
BLOCK = 128
LANES = 128
MESH = pl.DeviceIdType.MESH

rope_base = 1000000.0


def tables(row_count, key_total):
    half_width = HEAD // 2
    frequency = rope_base ** (-(jnp.arange(half_width, dtype=jnp.float32) * 2.0) / HEAD)
    positions = key_total - row_count + jnp.arange(row_count, dtype=jnp.int32)
    angles = positions.astype(jnp.float32)[:, None] * frequency[None, :]
    cosine = jnp.cos(angles) * HEAD ** (-0.5)
    sine = jnp.sin(angles) * HEAD ** (-0.5)
    return jnp.concatenate([cosine, cosine], axis=1), jnp.concatenate([-sine, sine], axis=1)


def low_bit(m):
    return m & -m


def high_bit(m):
    return 1 << (m.bit_length() - 1)


def route(mask, piece):
    return low_bit(mask) if piece % 2 == 0 else high_bit(mask)


def kernel(
    cfg,
    lists, tokens, wq, wo, kc, vc, cos_ref, sin_ref,
    out,
    tok, wq_buf, wo_buf, k_buf, v_buf, acc, qc, k_pick, v_pick, bias, recv_main, recv_dn,
    tok_sem, own_sem, send_sem, wq_sem, wo_sem, kv_send, kv_sem, rs_send, rs_sem, dn_sem, out_sem,
):
    n_f, n_c, nq, nw = cfg
    chips = n_f // 2
    bits = [1 << i for i in range(chips.bit_length() - 1)]
    masks = sorted(range(1, chips), key=lambda m: (bin(m).count("1"), m))
    f = lax.axis_index("fsdp")
    c = lax.axis_index("ctx")
    rows = tok.shape[1]
    depth = tok.shape[2]
    qcols = wq_buf.shape[2]
    qp = wq_buf.shape[1] // nq
    wp = depth // nw
    ratio = n_f // n_c
    blk_dev = kc.shape[0]
    kv_cols = k_buf.shape[2]
    kv_local = kv_cols // HEAD
    group = qcols // kv_cols
    n_blocks = k_buf.shape[0]
    q_blocks = rows // BLOCK
    n_list = lists.shape[2]

    def flip(x):
        bit, total = 1, 0
        while bit < n_f:
            total += lax.rem(lax.div(f, bit) + x // bit, 2) * bit
            bit *= 2
        return total

    def peer(x):
        return (flip(x), c)

    barrier = pltpu.get_barrier_semaphore()
    for x in [1] + [2 * b for b in bits]:
        pl.semaphore_signal(barrier, inc=1, device_id=peer(x), device_id_type=MESH)
    for d in range(1, n_c):
        pl.semaphore_signal(
            barrier, inc=1, device_id=(f, lax.rem(c + d, n_c)), device_id_type=MESH
        )
    pl.semaphore_wait(barrier, 1 + len(bits) + n_c - 1)

    sent = []

    def view(kind, ref, s):
        if kind == 0:
            return ref.at[pl.ds(s * qp, qp), :]
        return ref.at[:, pl.ds(s * wp, wp)]

    shard = (wq, wo)
    bufs = (wq_buf, wo_buf)
    sems = (wq_sem, wo_sem)
    counts = (nq, nw)

    def send(kind, src, slot, s, to):
        copy = pltpu.make_async_remote_copy(
            src_ref=src,
            dst_ref=view(kind, bufs[kind].at[slot], s),
            send_sem=send_sem.at[len(sent)],
            recv_sem=sems[kind].at[slot, s],
            device_id=peer(to),
            device_id_type=MESH,
        )
        copy.start()
        sent.append(copy)

    def arrived(kind, slot, s):
        pltpu.make_async_remote_copy(
            src_ref=view(kind, bufs[kind].at[slot], s),
            dst_ref=view(kind, bufs[kind].at[slot], s),
            send_sem=send_sem.at[0],
            recv_sem=sems[kind].at[slot, s],
            device_id=peer(1),
            device_id_type=MESH,
        ).wait_recv()

    stream = [(0, s) for s in range(nq)] + [(1, s) for s in range(nw)]

    def directs(i):
        if i < len(stream):
            kind, s = stream[i]
            for b in bits:
                send(kind, view(kind, shard[kind], s), 2 * b, s, 2 * b)

    def kv_copy(which, d):
        other = lax.rem(c + d, n_c)
        src, dst = ((kc, k_buf), (vc, v_buf))[which]
        return pltpu.make_async_remote_copy(
            src_ref=src.at[:, :, pl.ds(pl.multiple_of(other * kv_cols, LANES), kv_cols)],
            dst_ref=dst.at[pl.ds(c * blk_dev, blk_dev)],
            send_sem=kv_send.at[which, d],
            recv_sem=kv_sem.at[which, d],
            device_id=(f, other),
            device_id_type=MESH,
        )

    directs(0)
    for s in range(nq):
        send(0, view(0, wq, s), 1, s, 1)
    directs(1)

    def tok_copy(j):
        start = pl.multiple_of(flip(j) * depth, LANES)
        return pltpu.make_async_copy(tokens.at[:, pl.ds(start, depth)], tok.at[j], tok_sem.at[j])

    own_q = pltpu.make_async_copy(wq, wq_buf.at[0], own_sem.at[0])
    own_q.start()
    for j in range(n_f):
        tok_copy(j).start()
    kv_sent = []
    for d in range(1, n_c):
        for which in range(2):
            copy = kv_copy(which, d)
            copy.start()
            kv_sent.append(copy)
    mine = pl.ds(pl.multiple_of(c * kv_cols, LANES), kv_cols)
    own_k = pltpu.make_async_copy(kc.at[:, :, mine], k_buf.at[pl.ds(c * blk_dev, blk_dev)], own_sem.at[2])
    own_v = pltpu.make_async_copy(vc.at[:, :, mine], v_buf.at[pl.ds(c * blk_dev, blk_dev)], own_sem.at[3])
    own_k.start()
    own_v.start()
    own_o = pltpu.make_async_copy(wo, wo_buf.at[0], own_sem.at[1])
    own_o.start()
    for s in range(nw):
        send(1, view(1, wo, s), 1, s, 1)

    acc[...] = jnp.zeros_like(acc)
    tile = min(256, qcols)
    tiles = qcols // tile

    def q_piece(j, s):
        left = tok[j, :, s * qp:(s + 1) * qp]

        @pl.loop(0, tiles)
        def _(t):
            cols = pl.ds(pl.multiple_of(t * tile, tile), tile)
            acc[:, cols] += jnp.dot(
                left, wq_buf[j, s * qp:(s + 1) * qp, cols], preferred_element_type=jnp.float32
            )

    def q_whole(j):
        @pl.loop(0, tiles)
        def _(t):
            cols = pl.ds(pl.multiple_of(t * tile, tile), tile)
            acc[:, cols] += jnp.dot(tok[j], wq_buf[j, :, cols], preferred_element_type=jnp.float32)

    own_q.wait()
    for j in range(n_f):
        tok_copy(j).wait()
    for s in range(nq):
        arrived(0, 1, s)

    @pl.loop(0, 2)
    def _(j):
        q_whole(j)

    def pass_on(i):
        kind, s = stream[i]
        for m in masks:
            arrived(kind, 2 * m, s)
            piece = view(kind, bufs[kind].at[2 * m], s)
            for b in bits:
                if not (m & b) and route(m | b, s) == b:
                    send(kind, piece, 2 * (m | b), s, 2 * b)
            send(kind, piece, 2 * m + 1, s, 1)
            if m == bits[-1]:
                directs(i + 2)

    for s in range(nq):
        pass_on(s)

        @pl.loop(2, n_f)
        def _(j):
            @pl.when(lax.rem(j, 2) == 1)
            def _():
                arrived(0, j, s)

            q_piece(j, s)

    for h in range(qcols // HEAD):
        cols = slice(h * HEAD, (h + 1) * HEAD)
        x = acc[:, cols]
        turned = x * cos_ref[...] + pltpu.roll(x, HEAD // 2, 1) * sin_ref[...]
        qc[:, cols] = turned.astype(jnp.bfloat16)

    own_k.wait()
    own_v.wait()
    for copy in kv_sent:
        copy.wait_recv()

    @pl.loop(0, q_blocks)
    def _(b):
        q_rows = pl.ds(pl.multiple_of(b * BLOCK, BLOCK), BLOCK)
        own_block = n_blocks - q_blocks + b
        later = lax.broadcasted_iota(jnp.int32, (BLOCK, BLOCK), 1) > lax.broadcasted_iota(
            jnp.int32, (BLOCK, BLOCK), 0
        )
        for n in range(n_list):
            entry = lists[0, b, n]
            hide = jnp.where(entry == own_block, -jnp.inf, 0.0)
            bias[:, n * BLOCK:(n + 1) * BLOCK] = jnp.where(later, hide, 0.0)
        for g in range(kv_local):
            head_cols = slice(g * HEAD, (g + 1) * HEAD)
            for n in range(n_list):
                entry = lists[0, b, n]
                k_pick[n * BLOCK:(n + 1) * BLOCK, :] = k_buf[entry, :, head_cols]
                v_pick[n * BLOCK:(n + 1) * BLOCK, :] = v_buf[entry, :, head_cols]
            for i in range(group):
                h = g * group + i
                cols = slice(h * HEAD, (h + 1) * HEAD)
                scores = lax.dot_general(
                    qc[q_rows, cols], k_pick[...], (((1,), (1,)), ((), ())),
                    preferred_element_type=jnp.float32,
                ) + bias[...]
                top = jnp.max(scores, axis=1, keepdims=True)
                raised = jnp.exp(scores - top)
                total = jnp.sum(raised, axis=1, keepdims=True)
                mixed = jnp.dot(
                    raised.astype(jnp.bfloat16), v_pick[...], preferred_element_type=jnp.float32
                )
                qc[q_rows, cols] = (mixed / total).astype(jnp.bfloat16)

    last = n_c - 1

    def place(j):
        target = flip(j)
        return lax.div(target, ratio), lax.rem(target, ratio)

    def rs_copy(j, s, to_dn):
        dst, part = place(j)
        cols = pl.ds(s * wp, wp)
        nxt = jnp.where(c < dst, c + 1, c - 1)
        return pltpu.make_async_remote_copy(
            src_ref=tok.at[j, :, cols],
            dst_ref=recv_dn.at[part, :, cols] if to_dn else recv_main.at[j, :, cols],
            send_sem=rs_send.at[j, s],
            recv_sem=dn_sem.at[part, s] if to_dn else rs_sem.at[j, s],
            device_id=(f, nxt),
            device_id_type=MESH,
        )

    def rs_start(j, s):
        dst, _ = place(j)

        @pl.when(c == dst + 1)
        def _():
            rs_copy(j, s, True).start()

        @pl.when(c != dst + 1)
        def _():
            rs_copy(j, s, False).start()

    def share(j, s):
        cols = slice(s * wp, (s + 1) * wp)
        tok[j, :, cols] = jnp.dot(
            qc[...], wo_buf[j, :, cols], preferred_element_type=jnp.float32
        ).astype(jnp.bfloat16)
        dst, _ = place(j)

        @pl.when(jnp.logical_and(c != dst, jnp.logical_or(c == 0, c == last)))
        def _():
            rs_start(j, s)

    def out_copy(j, s):
        _, part = place(j)
        start = pl.multiple_of(part * depth + s * wp, LANES)
        return pltpu.make_async_copy(
            tok.at[j, :, pl.ds(s * wp, wp)], out.at[:, pl.ds(start, wp)], out_sem.at[part, s]
        )

    def progress(j, s):
        dst, part = place(j)
        cols = slice(s * wp, (s + 1) * wp)
        middle = jnp.logical_and(c > 0, c < last)
        is_dst = c == dst

        def f32(x):
            return x.astype(jnp.float32)

        @pl.when(jnp.logical_and(middle, jnp.logical_not(is_dst)))
        def _():
            rs_copy(j, s, False).wait_recv()
            tok[j, :, cols] = (f32(tok[j, :, cols]) + f32(recv_main[j, :, cols])).astype(jnp.bfloat16)
            rs_start(j, s)

        @pl.when(is_dst)
        def _():
            @pl.when(c > 0)
            def _():
                rs_copy(j, s, False).wait_recv()

            @pl.when(c < last)
            def _():
                rs_copy(j, s, True).wait_recv()

            @pl.when(c == 0)
            def _():
                tok[j, :, cols] = (f32(tok[j, :, cols]) + f32(recv_dn[part, :, cols])).astype(jnp.bfloat16)

            @pl.when(c == last)
            def _():
                tok[j, :, cols] = (f32(tok[j, :, cols]) + f32(recv_main[j, :, cols])).astype(jnp.bfloat16)

            @pl.when(middle)
            def _():
                tok[j, :, cols] = (
                    f32(tok[j, :, cols]) + f32(recv_main[j, :, cols]) + f32(recv_dn[part, :, cols])
                ).astype(jnp.bfloat16)

            out_copy(j, s).start()

    own_o.wait()
    for s in range(nw):
        arrived(1, 1, s)
    for s in range(nw):
        @pl.loop(0, 2)
        def _(j):
            share(j, s)

    for s in range(nw):
        pass_on(nq + s)

        @pl.loop(2, n_f)
        def _(j):
            @pl.when(lax.rem(j, 2) == 1)
            def _():
                arrived(1, j, s)

            share(j, s)

        if s == 0:
            for t in range(nw):
                @pl.loop(0, 2)
                def _(j):
                    progress(j, t)
        else:
            @pl.loop(2, n_f)
            def _(j):
                progress(j, s - 1)

    @pl.loop(2, n_f)
    def _(j):
        progress(j, nw - 1)

    assert len(sent) == send_sem.shape[0]
    for copy in sent + kv_sent:
        copy.wait_send()
    for s in range(nw):
        @pl.loop(0, n_f)
        def _(j):
            dst, _ = place(j)

            @pl.when(c == dst)
            def _():
                out_copy(j, s).wait()

            @pl.when(c != dst)
            def _():
                rs_copy(j, s, False).wait_send()


def body(n_f, n_c, tokens, wq, wo, key_cache, value_cache, key_blocks):
    rows, width = tokens.shape
    depth = width // n_f
    qcols = wq.shape[1]
    cache = key_cache.shape[0]
    blk_dev = cache // BLOCK
    kv_cols = key_cache.shape[1] // n_c
    n_list = key_blocks.shape[2]
    cosine, sine = tables(rows, cache * n_c)
    nq = max(1, min(4, wq.shape[0] // LANES))
    nw = max(1, min(4, wo.shape[1] // LANES))
    any_spec = pl.BlockSpec(memory_space=pl.ANY)
    vmem_spec = pl.BlockSpec(memory_space=pltpu.VMEM)
    ratio = n_f // n_c
    bf16 = jnp.bfloat16
    dma = pltpu.SemaphoreType.DMA
    return pl.pallas_call(
        functools.partial(kernel, (n_f, n_c, nq, nw)),
        out_shape=jax.ShapeDtypeStruct((rows, width // n_c), bf16),
        in_specs=[pl.BlockSpec(memory_space=pltpu.SMEM)] + [any_spec] * 5 + [vmem_spec] * 2,
        out_specs=any_spec,
        scratch_shapes=[
            pltpu.VMEM((n_f, rows, depth), bf16),
            pltpu.VMEM((n_f,) + wq.shape, bf16),
            pltpu.VMEM((n_f,) + wo.shape, bf16),
            pltpu.VMEM((blk_dev * n_c, BLOCK, kv_cols), bf16),
            pltpu.VMEM((blk_dev * n_c, BLOCK, kv_cols), bf16),
            pltpu.VMEM((rows, qcols), jnp.float32),
            pltpu.VMEM((rows, qcols), bf16),
            pltpu.VMEM((n_list * BLOCK, HEAD), bf16),
            pltpu.VMEM((n_list * BLOCK, HEAD), bf16),
            pltpu.VMEM((BLOCK, n_list * BLOCK), jnp.float32),
            pltpu.VMEM((n_f, rows, depth), bf16),
            pltpu.VMEM((ratio, rows, depth), bf16),
            dma((n_f,)),
            dma((4,)),
            dma(((nq + nw) * (n_f - 1),)),
            dma((n_f, nq)),
            dma((n_f, nw)),
            dma((2, n_c)),
            dma((2, n_c)),
            dma((n_f, nw)),
            dma((n_f, nw)),
            dma((ratio, nw)),
            dma((ratio, nw)),
        ],
        compiler_params=pltpu.CompilerParams(
            collective_id=0, has_side_effects=True, vmem_limit_bytes=67043328
        ),
    )(
        key_blocks,
        tokens,
        wq,
        wo,
        key_cache.reshape(blk_dev, BLOCK, key_cache.shape[1]),
        value_cache.reshape(blk_dev, BLOCK, value_cache.shape[1]),
        cosine,
        sine,
    )


def solution(mesh):
    in_specs = (
        P("fsdp", None),
        P("fsdp", "ctx"),
        P("ctx", "fsdp"),
        P(("fsdp", "ctx"), None),
        P(("fsdp", "ctx"), None),
        P("fsdp", None, None),
    )
    step = functools.partial(body, mesh.shape["fsdp"], mesh.shape["ctx"])
    return jax.shard_map(
        step, mesh=mesh, in_specs=in_specs, out_specs=P("fsdp", "ctx"), check_vma=False
    )
```

time: 362 us -> 381 us (1.052)
  the two profiles are of different devices: /device:TPU:29 before, /device:TPU:6 now
where the time goes in v1:
time: 381 us
  Pallas kernels  375 us (98%)
    pallas_call x1, Pallas kernels, body(): pl.pallas_call(functools.partial(kernel, (n_f, n_c, nq, nw)), out_shape=j...  375 us

profile of v1, /device:TPU:6, one launch (start us, length us, event | category | flops | bytes accessed | tf_op | source)
XLA Modules:
  0.0 380.6 jit_solution(10512864354837070116)
XLA Ops:
  0.0 1.0 fusion.2
  1.0 1.0 pad_maximum_fusion
  2.1 375.4 %shard_map.64 = bf16[512,2048]{1,0:T(8,128)(2,1)} custom-call(s32[1,4,8]{2,1,0:T(4,128)} %lists.1, bf16[512,8192]{1,0:T(8,128)(2,1)} %tokens.1, bf16[1024,1024]{1,0:T(8,128)(2,1)} %wq.1, bf16[1024,1024]{1,0:T(8,128)(2,1)} %wo.1, bf16[2,128,1024]{2,1,0:T(8,128)(2,1)} %bitcast.2, bf16[2,128,1024]{2,1,0:T(8,128)(2,1)} %bitcast.3, ...), custom_call_target="tpu_custom_call" | custom-call | tf_op jit(solution)/shard_map/pallas_call | solution.py:420
  377.4 3.2 copy.8
  (2 shorter events, 0.0 us)

commit v2 on v1

--- a/solution.py
+++ b/solution.py
@@ -10,6 +10,7 @@
 HEAD = 128
 BLOCK = 128
 LANES = 128
+AHEAD = 2
 MESH = pl.DeviceIdType.MESH
 
 rope_base = 1000000.0
@@ -41,8 +42,9 @@
     cfg,
     lists, tokens, wq, wo, kc, vc, cos_ref, sin_ref,
     out,
-    tok, wq_buf, wo_buf, k_buf, v_buf, acc, qc, k_pick, v_pick, bias, recv_main, recv_dn,
-    tok_sem, own_sem, send_sem, wq_sem, wo_sem, kv_send, kv_sem, rs_send, rs_sem, dn_sem, out_sem,
+    tok, wq_buf, wo_buf, k_buf, v_buf, acc, qc, k_pick, v_pick, bias, ctx_all, ctx_perm, staged,
+    tok_sem, own_sem, send_sem, wq_sem, wo_sem, kv_send, kv_sem, ctx_send, ctx_sem,
+    move_send, move_sem, out_sem,
 ):
     n_f, n_c, nq, nw = cfg
     chips = n_f // 2
@@ -54,7 +56,9 @@
     depth = tok.shape[2]
     qcols = wq_buf.shape[2]
     qp = wq_buf.shape[1] // nq
-    wp = depth // nw
+    wo_cols = wo.shape[1]
+    wp = wo_buf.shape[2] // nw
+    part = wo.shape[0] // chips
     ratio = n_f // n_c
     blk_dev = kc.shape[0]
     kv_cols = k_buf.shape[2]
@@ -75,13 +79,16 @@
         return (flip(x), c)
 
     barrier = pltpu.get_barrier_semaphore()
-    for x in [1] + [2 * b for b in bits]:
-        pl.semaphore_signal(barrier, inc=1, device_id=peer(x), device_id_type=MESH)
-    for d in range(1, n_c):
+    me = f * n_c + c
+
+    @pl.loop(1, n_f * n_c)
+    def _(d):
+        other = lax.rem(me + d, n_f * n_c)
         pl.semaphore_signal(
-            barrier, inc=1, device_id=(f, lax.rem(c + d, n_c)), device_id_type=MESH
-        )
-    pl.semaphore_wait(barrier, 1 + len(bits) + n_c - 1)
+            barrier, inc=1, device_id=(lax.div(other, n_c), lax.rem(other, n_c)), device_id_type=MESH
+        )
+
+    pl.semaphore_wait(barrier, n_f * n_c - 1)
 
     sent = []
 
@@ -90,7 +97,7 @@
             return ref.at[pl.ds(s * qp, qp), :]
         return ref.at[:, pl.ds(s * wp, wp)]
 
-    shard = (wq, wo)
+    shard = (wq, wo_buf.at[0])
     bufs = (wq_buf, wo_buf)
     sems = (wq_sem, wo_sem)
     counts = (nq, nw)
@@ -161,10 +168,69 @@
     own_v = pltpu.make_async_copy(vc.at[:, :, mine], v_buf.at[pl.ds(c * blk_dev, blk_dev)], own_sem.at[3])
     own_k.start()
     own_v.start()
-    own_o = pltpu.make_async_copy(wo, wo_buf.at[0], own_sem.at[1])
-    own_o.start()
-    for s in range(nw):
-        send(1, view(1, wo, s), 1, s, 1)
+
+    core = lax.rem(f, 2)
+    home = lax.div(f, ratio)
+    block = lax.div(lax.rem(f, ratio), 2)
+
+    def move_dst(i, plane):
+        return wo_buf.at[
+            0,
+            pl.ds(pl.multiple_of(plane * part, part), part),
+            pl.ds(pl.multiple_of(i * wo_cols, wo_cols), wo_cols),
+        ]
+
+    def move(q):
+        return pltpu.make_async_remote_copy(
+            src_ref=wo.at[pl.ds(pl.multiple_of(q * part, part), part), :],
+            dst_ref=move_dst(block, c),
+            send_sem=move_send.at[q],
+            recv_sem=move_sem.at[block, c],
+            device_id=(q * 2 + core, home),
+            device_id_type=MESH,
+        )
+
+    def keep(q):
+        return pltpu.make_async_copy(
+            wo.at[pl.ds(pl.multiple_of(q * part, part), part), :], move_dst(block, c), own_sem.at[1]
+        )
+
+    def stays(q):
+        return jnp.logical_and(home == c, lax.div(f, 2) == q)
+
+    def start_moves():
+        @pl.loop(0, chips)
+        def _(d):
+            q = lax.rem(lax.div(f, 2) + d, chips)
+
+            @pl.when(stays(q))
+            def _():
+                keep(q).start()
+
+            @pl.when(jnp.logical_not(stays(q)))
+            def _():
+                move(q).start()
+
+    def wait_moves():
+        for i in range(ratio // 2):
+            @pl.loop(0, n_c)
+            def _(plane):
+                own = jnp.logical_and(home == c, jnp.logical_and(plane == c, block == i))
+
+                @pl.when(own)
+                def _():
+                    keep(lax.div(f, 2)).wait()
+
+                @pl.when(jnp.logical_not(own))
+                def _():
+                    pltpu.make_async_remote_copy(
+                        src_ref=move_dst(i, plane),
+                        dst_ref=move_dst(i, plane),
+                        send_sem=move_send.at[0],
+                        recv_sem=move_sem.at[i, plane],
+                        device_id=peer(1),
+                        device_id_type=MESH,
+                    ).wait_recv()
 
     acc[...] = jnp.zeros_like(acc)
     tile = min(256, qcols)
@@ -205,11 +271,21 @@
                 if not (m & b) and route(m | b, s) == b:
                     send(kind, piece, 2 * (m | b), s, 2 * b)
             send(kind, piece, 2 * m + 1, s, 1)
-            if m == bits[-1]:
+            if m == bits[-1] and kind == 0 and i + 2 < nq:
                 directs(i + 2)
+            if m == bits[-1] and kind == 1:
+                directs(i + AHEAD)
 
     for s in range(nq):
         pass_on(s)
+        if s == max(0, nq - 3):
+            start_moves()
+        if s == nq - 1:
+            wait_moves()
+            for i in range(AHEAD):
+                directs(nq + i)
+            for i in range(nw):
+                send(1, view(1, shard[1], i), 1, i, 1)
 
         @pl.loop(2, n_f)
         def _(j):
@@ -229,6 +305,17 @@
     own_v.wait()
     for copy in kv_sent:
         copy.wait_recv()
+
+    def ctx_copy(b, d):
+        q_rows = pl.ds(pl.multiple_of(b * BLOCK, BLOCK), BLOCK)
+        return pltpu.make_async_remote_copy(
+            src_ref=qc.at[q_rows],
+            dst_ref=ctx_all.at[c, q_rows],
+            send_sem=ctx_send.at[b, d],
+            recv_sem=ctx_sem.at[b, d],
+            device_id=(f, lax.rem(c + d, n_c)),
+            device_id_type=MESH,
+        )
 
     @pl.loop(0, q_blocks)
     def _(b):
@@ -262,107 +349,43 @@
                 )
                 qc[q_rows, cols] = (mixed / total).astype(jnp.bfloat16)
 
-    last = n_c - 1
-
-    def place(j):
+        @pl.loop(1, n_c)
+        def _(d):
+            ctx_copy(b, d).start()
+
+    acc[...] = jnp.zeros_like(acc)
+
+    def share(j, s):
         target = flip(j)
-        return lax.div(target, ratio), lax.rem(target, ratio)
-
-    def rs_copy(j, s, to_dn):
-        dst, part = place(j)
-        cols = pl.ds(s * wp, wp)
-        nxt = jnp.where(c < dst, c + 1, c - 1)
-        return pltpu.make_async_remote_copy(
-            src_ref=tok.at[j, :, cols],
-            dst_ref=recv_dn.at[part, :, cols] if to_dn else recv_main.at[j, :, cols],
-            send_sem=rs_send.at[j, s],
-            recv_sem=dn_sem.at[part, s] if to_dn else rs_sem.at[j, s],
-            device_id=(f, nxt),
-            device_id_type=MESH,
-        )
-
-    def rs_start(j, s):
-        dst, _ = place(j)
-
-        @pl.when(c == dst + 1)
-        def _():
-            rs_copy(j, s, True).start()
-
-        @pl.when(c != dst + 1)
-        def _():
-            rs_copy(j, s, False).start()
-
-    def share(j, s):
-        cols = slice(s * wp, (s + 1) * wp)
-        tok[j, :, cols] = jnp.dot(
-            qc[...], wo_buf[j, :, cols], preferred_element_type=jnp.float32
-        ).astype(jnp.bfloat16)
-        dst, _ = place(j)
-
-        @pl.when(jnp.logical_and(c != dst, jnp.logical_or(c == 0, c == last)))
-        def _():
-            rs_start(j, s)
-
-    def out_copy(j, s):
-        _, part = place(j)
-        start = pl.multiple_of(part * depth + s * wp, LANES)
-        return pltpu.make_async_copy(
-            tok.at[j, :, pl.ds(s * wp, wp)], out.at[:, pl.ds(start, wp)], out_sem.at[part, s]
-        )
-
-    def progress(j, s):
-        dst, part = place(j)
-        cols = slice(s * wp, (s + 1) * wp)
-        middle = jnp.logical_and(c > 0, c < last)
-        is_dst = c == dst
-
-        def f32(x):
-            return x.astype(jnp.float32)
-
-        @pl.when(jnp.logical_and(middle, jnp.logical_not(is_dst)))
-        def _():
-            rs_copy(j, s, False).wait_recv()
-            tok[j, :, cols] = (f32(tok[j, :, cols]) + f32(recv_main[j, :, cols])).astype(jnp.bfloat16)
-            rs_start(j, s)
-
-        @pl.when(is_dst)
-        def _():
-            @pl.when(c > 0)
-            def _():
-                rs_copy(j, s, False).wait_recv()
-
-            @pl.when(c < last)
-            def _():
-                rs_copy(j, s, True).wait_recv()
-
-            @pl.when(c == 0)
-            def _():
-                tok[j, :, cols] = (f32(tok[j, :, cols]) + f32(recv_dn[part, :, cols])).astype(jnp.bfloat16)
-
-            @pl.when(c == last)
-            def _():
-                tok[j, :, cols] = (f32(tok[j, :, cols]) + f32(recv_main[j, :, cols])).astype(jnp.bfloat16)
-
-            @pl.when(middle)
-            def _():
-                tok[j, :, cols] = (
-                    f32(tok[j, :, cols]) + f32(recv_main[j, :, cols]) + f32(recv_dn[part, :, cols])
-                ).astype(jnp.bfloat16)
-
-            out_copy(j, s).start()
-
-    own_o.wait()
-    for s in range(nw):
-        arrived(1, 1, s)
-    for s in range(nw):
-        @pl.loop(0, 2)
-        def _(j):
-            share(j, s)
+        i, offset = divmod(s * wp, wo_cols)
+        start = pl.multiple_of((2 * i + lax.rem(target, 2)) * wo_cols + offset, LANES)
+        acc[:, pl.ds(start, wp)] += jnp.dot(
+            ctx_perm[lax.div(target, 2)], wo_buf[j, :, s * wp:(s + 1) * wp],
+            preferred_element_type=jnp.float32,
+        )
+
+    def out_copy(s, k):
+        i, offset = divmod(s * wp, wo_cols)
+        cols = pl.ds((2 * i + k) * wo_cols + offset, wp)
+        return pltpu.make_async_copy(staged.at[:, cols], out.at[:, cols], out_sem.at[s, k])
 
     for s in range(nw):
         pass_on(nq + s)
-
-        @pl.loop(2, n_f)
+    ctx_all[c] = qc[...]
+
+    @pl.loop(0, q_blocks)
+    def _(b):
+        @pl.loop(1, n_c)
+        def _(d):
+            ctx_copy(b, d).wait_recv()
+
+    for q in range(chips):
+        for plane in range(n_c):
+            ctx_perm[q, :, plane * part:(plane + 1) * part] = ctx_all[
+                plane, :, q * part:(q + 1) * part
+            ]
+    for s in range(nw):
+        @pl.loop(0, n_f)
         def _(j):
             @pl.when(lax.rem(j, 2) == 1)
             def _():
@@ -370,35 +393,31 @@
 
             share(j, s)
 
-        if s == 0:
-            for t in range(nw):
-                @pl.loop(0, 2)
-                def _(j):
-                    progress(j, t)
-        else:
-            @pl.loop(2, n_f)
-            def _(j):
-                progress(j, s - 1)
-
-    @pl.loop(2, n_f)
-    def _(j):
-        progress(j, nw - 1)
+        for k in range(2):
+            i, offset = divmod(s * wp, wo_cols)
+            cols = pl.ds((2 * i + k) * wo_cols + offset, wp)
+            staged[:, cols] = acc[:, cols].astype(jnp.bfloat16)
+            out_copy(s, k).start()
 
     assert len(sent) == send_sem.shape[0]
     for copy in sent + kv_sent:
         copy.wait_send()
+
+    @pl.loop(0, q_blocks)
+    def _(b):
+        @pl.loop(1, n_c)
+        def _(d):
+            ctx_copy(b, d).wait_send()
+
+    @pl.loop(0, chips)
+    def _(q):
+        @pl.when(jnp.logical_not(stays(q)))
+        def _():
+            move(q).wait_send()
+
     for s in range(nw):
-        @pl.loop(0, n_f)
-        def _(j):
-            dst, _ = place(j)
-
-            @pl.when(c == dst)
-            def _():
-                out_copy(j, s).wait()
-
-            @pl.when(c != dst)
-            def _():
-                rs_copy(j, s, False).wait_send()
+        for k in range(2):
+            out_copy(s, k).wait()
 
 
 def body(n_f, n_c, tokens, wq, wo, key_cache, value_cache, key_blocks):
@@ -411,10 +430,13 @@
     n_list = key_blocks.shape[2]
     cosine, sine = tables(rows, cache * n_c)
     nq = max(1, min(4, wq.shape[0] // LANES))
-    nw = max(1, min(4, wo.shape[1] // LANES))
+    ratio = n_f // n_c
+    chips = n_f // 2
+    part = wo.shape[0] // chips
+    moved = (part * n_c, wo.shape[1] * ratio // 2)
+    nw = max(1, min(4, moved[1] // LANES))
     any_spec = pl.BlockSpec(memory_space=pl.ANY)
     vmem_spec = pl.BlockSpec(memory_space=pltpu.VMEM)
-    ratio = n_f // n_c
     bf16 = jnp.bfloat16
     dma = pltpu.SemaphoreType.DMA
     return pl.pallas_call(
@@ -425,16 +447,17 @@
         scratch_shapes=[
             pltpu.VMEM((n_f, rows, depth), bf16),
             pltpu.VMEM((n_f,) + wq.shape, bf16),
-            pltpu.VMEM((n_f,) + wo.shape, bf16),
+            pltpu.VMEM((n_f,) + moved, bf16),
             pltpu.VMEM((blk_dev * n_c, BLOCK, kv_cols), bf16),
             pltpu.VMEM((blk_dev * n_c, BLOCK, kv_cols), bf16),
-            pltpu.VMEM((rows, qcols), jnp.float32),
+            pltpu.VMEM((rows, max(qcols, width // n_c)), jnp.float32),
             pltpu.VMEM((rows, qcols), bf16),
             pltpu.VMEM((n_list * BLOCK, HEAD), bf16),
             pltpu.VMEM((n_list * BLOCK, HEAD), bf16),
             pltpu.VMEM((BLOCK, n_list * BLOCK), jnp.float32),
-            pltpu.VMEM((n_f, rows, depth), bf16),
-            pltpu.VMEM((ratio, rows, depth), bf16),
+            pltpu.VMEM((n_c, rows, qcols), bf16),
+            pltpu.VMEM((chips, rows, n_c * part), bf16),
+            pltpu.VMEM((rows, width // n_c), bf16),
             dma((n_f,)),
             dma((4,)),
             dma(((nq + nw) * (n_f - 1),)),
@@ -442,10 +465,11 @@
             dma((n_f, nw)),
             dma((2, n_c)),
             dma((2, n_c)),
-            dma((n_f, nw)),
-            dma((n_f, nw)),
-            dma((ratio, nw)),
-            dma((ratio, nw)),
+            dma((rows // BLOCK, n_c)),
+            dma((rows // BLOCK, n_c)),
+            dma((chips,)),
+            dma((ratio // 2, n_c)),
+            dma((nw, 2)),
         ],
         compiler_params=pltpu.CompilerParams(
             collective_id=0, has_side_effects=True, vmem_limit_bytes=67043328

time: 381 us -> 336 us (0.88)
  the two profiles are of different devices: /device:TPU:6 before, /device:TPU:0 now
where the time goes in v2:
time: 336 us
  Pallas kernels  330 us (98%)
    pallas_call x1, Pallas kernels, body(): pl.pallas_call(functools.partial(kernel, (n_f, n_c, nq, nw)), out_shape=j...  330 us

profile of v2, /device:TPU:0, one launch (start us, length us, event | category | flops | bytes accessed | tf_op | source)
XLA Modules:
  0.0 335.6 jit_solution(9709384413495797644)
XLA Ops:
  0.0 1.0 fusion.2
  1.0 1.0 pad_maximum_fusion
  2.1 330.3 %shard_map.64 = bf16[512,2048]{1,0:T(8,128)(2,1)} custom-call(s32[1,4,8]{2,1,0:T(4,128)} %lists.1, bf16[512,8192]{1,0:T(8,128)(2,1)} %tokens.1, bf16[1024,1024]{1,0:T(8,128)(2,1)} %wq.1, bf16[1024,1024]{1,0:T(8,128)(2,1)} %wo.1, bf16[2,128,1024]{2,1,0:T(8,128)(2,1)} %bitcast.2, bf16[2,128,1024]{2,1,0:T(8,128)(2,1)} %bitcast.3, ...), custom_call_target="tpu_custom_call" | custom-call | tf_op jit(solution)/shard_map/pallas_call | solution.py:442
  332.4 3.2 copy.8
  (2 shorter events, 0.0 us)

commit v3 on v2

--- a/solution.py
+++ b/solution.py
@@ -10,7 +10,7 @@
 HEAD = 128
 BLOCK = 128
 LANES = 128
-AHEAD = 2
+AHEAD = 3
 MESH = pl.DeviceIdType.MESH
 
 rope_base = 1000000.0
@@ -42,9 +42,9 @@
     cfg,
     lists, tokens, wq, wo, kc, vc, cos_ref, sin_ref,
     out,
-    tok, wq_buf, wo_buf, k_buf, v_buf, acc, qc, k_pick, v_pick, bias, ctx_all, ctx_perm, staged,
+    tok, wq_buf, wo_buf, k_buf, v_buf, acc, qc, k_pick, v_pick, bias, ctx_all, ctx_perm, staged, hop,
     tok_sem, own_sem, send_sem, wq_sem, wo_sem, kv_send, kv_sem, ctx_send, ctx_sem,
-    move_send, move_sem, out_sem,
+    move_send, move_sem, keep_sem, hop_send, hop_sem, out_sem,
 ):
     n_f, n_c, nq, nw = cfg
     chips = n_f // 2
@@ -144,6 +144,90 @@
             device_id_type=MESH,
         )
 
+    core = lax.rem(f, 2)
+    chip = lax.div(f, 2)
+
+    def piece(q):
+        return wo.at[pl.ds(pl.multiple_of(q * part, part), part), :]
+
+    def hop_copy(q, source):
+        return pltpu.make_async_remote_copy(
+            src_ref=piece(q),
+            dst_ref=hop.at[source],
+            send_sem=hop_send.at[q],
+            recv_sem=hop_sem.at[source],
+            device_id=(q * 2 + core, c),
+            device_id_type=MESH,
+        )
+
+    def move_dst(i, plane):
+        return wo_buf.at[
+            0,
+            pl.ds(pl.multiple_of(plane * part, part), part),
+            pl.ds(pl.multiple_of(i * wo_cols, wo_cols), wo_cols),
+        ]
+
+    def owner(p):
+        source = p * 2 + core
+        return lax.div(source, ratio), lax.div(lax.rem(source, ratio), 2)
+
+    def move(src, p):
+        home, i = owner(p)
+        return pltpu.make_async_remote_copy(
+            src_ref=src,
+            dst_ref=move_dst(i, c),
+            send_sem=move_send.at[p],
+            recv_sem=move_sem.at[i, c],
+            device_id=(f, home),
+            device_id_type=MESH,
+        )
+
+    def keep(src, p):
+        _, i = owner(p)
+        return pltpu.make_async_copy(src, move_dst(i, c), keep_sem.at[i])
+
+    def start_hops():
+        @pl.loop(1, chips)
+        def _(d):
+            hop_copy(lax.rem(chip + d, chips), chip).start()
+
+    def forward(src, p):
+        home, _ = owner(p)
+
+        @pl.when(home == c)
+        def _():
+            keep(src, p).start()
+
+        @pl.when(home != c)
+        def _():
+            move(src, p).start()
+
+    def start_moves():
+        forward(piece(chip), chip)
+
+        @pl.loop(1, chips)
+        def _(d):
+            p = lax.rem(chip + d, chips)
+            hop_copy(p, p).wait_recv()
+            forward(hop.at[p], p)
+
+    def wait_moves():
+        for i in range(ratio // 2):
+            keep(piece(chip), lax.div(c * ratio + 2 * i, 2)).wait()
+
+            @pl.loop(1, n_c)
+            def _(d):
+                plane = lax.rem(c + d, n_c)
+                pltpu.make_async_remote_copy(
+                    src_ref=move_dst(i, plane),
+                    dst_ref=move_dst(i, plane),
+                    send_sem=move_send.at[0],
+                    recv_sem=move_sem.at[i, plane],
+                    device_id=peer(1),
+                    device_id_type=MESH,
+                ).wait_recv()
+
+    start_hops()
     directs(0)
     for s in range(nq):
         send(0, view(0, wq, s), 1, s, 1)
@@ -169,69 +253,6 @@
     own_k.start()
     own_v.start()
 
-    core = lax.rem(f, 2)
-    home = lax.div(f, ratio)
-    block = lax.div(lax.rem(f, ratio), 2)
-
-    def move_dst(i, plane):
-        return wo_buf.at[
-            0,
-            pl.ds(pl.multiple_of(plane * part, part), part),
-            pl.ds(pl.multiple_of(i * wo_cols, wo_cols), wo_cols),
-        ]
-
-    def move(q):
-        return pltpu.make_async_remote_copy(
-            src_ref=wo.at[pl.ds(pl.multiple_of(q * part, part), part), :],
-            dst_ref=move_dst(block, c),
-            send_sem=move_send.at[q],
-            recv_sem=move_sem.at[block, c],
-            device_id=(q * 2 + core, home),
-            device_id_type=MESH,
-        )
-
-    def keep(q):
-        return pltpu.make_async_copy(
-            wo.at[pl.ds(pl.multiple_of(q * part, part), part), :], move_dst(block, c), own_sem.at[1]
-        )
-
-    def stays(q):
-        return jnp.logical_and(home == c, lax.div(f, 2) == q)
-
-    def start_moves():
-        @pl.loop(0, chips)
-        def _(d):
-            q = lax.rem(lax.div(f, 2) + d, chips)
-
-            @pl.when(stays(q))
-            def _():
-                keep(q).start()
-
-            @pl.when(jnp.logical_not(stays(q)))
-            def _():
-                move(q).start()
-
-    def wait_moves():
-        for i in range(ratio // 2):
-            @pl.loop(0, n_c)
-            def _(plane):
-                own = jnp.logical_and(home == c, jnp.logical_and(plane == c, block == i))
-
-                @pl.when(own)
-                def _():
-                    keep(lax.div(f, 2)).wait()
-
-                @pl.when(jnp.logical_not(own))
-                def _():
-                    pltpu.make_async_remote_copy(
-                        src_ref=move_dst(i, plane),
-                        dst_ref=move_dst(i, plane),
-                        send_sem=move_send.at[0],
-                        recv_sem=move_sem.at[i, plane],
-                        device_id=peer(1),
-                        device_id_type=MESH,
-                    ).wait_recv()
-
     acc[...] = jnp.zeros_like(acc)
     tile = min(256, qcols)
     tiles = qcols // tile
@@ -278,14 +299,16 @@
 
     for s in range(nq):
         pass_on(s)
-        if s == max(0, nq - 3):
+        if s == 0:
             start_moves()
-        if s == nq - 1:
+        if s == max(0, nq - 2):
             wait_moves()
-            for i in range(AHEAD):
-                directs(nq + i)
+            directs(nq)
             for i in range(nw):
                 send(1, view(1, shard[1], i), 1, i, 1)
+        if s == nq - 1:
+            for i in range(1, AHEAD):
+                directs(nq + i)
 
         @pl.loop(2, n_f)
         def _(j):
@@ -411,9 +434,15 @@
 
     @pl.loop(0, chips)
     def _(q):
-        @pl.when(jnp.logical_not(stays(q)))
+        @pl.when(q != chip)
         def _():
-            move(q).wait_send()
+            hop_copy(q, chip).wait_send()
+
+        home, _ = owner(q)
+
+        @pl.when(home != c)
+        def _():
+            move(piece(chip), q).wait_send()
 
     for s in range(nw):
         for k in range(2):
@@ -458,6 +487,7 @@
             pltpu.VMEM((n_c, rows, qcols), bf16),
             pltpu.VMEM((chips, rows, n_c * part), bf16),
             pltpu.VMEM((rows, width // n_c), bf16),
+            pltpu.VMEM((chips, part, wo.shape[1]), bf16),
             dma((n_f,)),
             dma((4,)),
             dma(((nq + nw) * (n_f - 1),)),
@@ -469,6 +499,9 @@
             dma((rows // BLOCK, n_c)),
             dma((chips,)),
             dma((ratio // 2, n_c)),
+            dma((ratio // 2,)),
+            dma((chips,)),
+            dma((chips,)),
             dma((nw, 2)),
         ],
         compiler_params=pltpu.CompilerParams(

time: 336 us -> 252 us (0.75)
  the two profiles are of different devices: /device:TPU:0 before, /device:TPU:29 now
where the time goes in v3:
time: 252 us
  Pallas kernels  246 us (98%)
  local copies, waits for them, and re-layouts  3.16 us (1%)
    pallas_call x1, Pallas kernels, body(): pl.pallas_call(functools.partial(kernel, (n_f, n_c, nq, nw)), out_shape=j...  246 us

profile of v3, /device:TPU:29, one launch (start us, length us, event | category | flops | bytes accessed | tf_op | source)
XLA Modules:
  0.0 251.7 jit_solution(6638454856670376888)
XLA Ops:
  0.0 1.0 fusion.2
  1.0 1.0 pad_maximum_fusion
  2.1 246.4 %shard_map.64 = bf16[512,2048]{1,0:T(8,128)(2,1)} custom-call(s32[1,4,8]{2,1,0:T(4,128)} %lists.1, bf16[512,8192]{1,0:T(8,128)(2,1)} %tokens.1, bf16[1024,1024]{1,0:T(8,128)(2,1)} %wq.1, bf16[1024,1024]{1,0:T(8,128)(2,1)} %wo.1, bf16[2,128,1024]{2,1,0:T(8,128)(2,1)} %bitcast.2, bf16[2,128,1024]{2,1,0:T(8,128)(2,1)} %bitcast.3, ...), custom_call_target="tpu_custom_call" | custom-call | tf_op jit(solution)/shard_map/pallas_call | solution.py:471
  248.5 3.2 %copy.8 = bf16[512,2048]{1,0:T(8,128)(2,1)} copy(bf16[512,2048]{1,0:T(8,128)(2,1)} %shard_map.64) | data formatting | bytes 4194304
  (2 shorter events, 0.0 us)

commit v4 on v3

--- a/solution.py
+++ b/solution.py
@@ -10,7 +10,7 @@
 HEAD = 128
 BLOCK = 128
 LANES = 128
-AHEAD = 3
+AHEAD = 4
 MESH = pl.DeviceIdType.MESH
 
 rope_base = 1000000.0

time: 252 us -> 252 us (level)
  no operation moved by 1% of the time
where the time goes in v4:
time: 252 us
  Pallas kernels  246 us (98%)
  local copies, waits for them, and re-layouts  3.16 us (1%)
    pallas_call x1, Pallas kernels, body(): pl.pallas_call(functools.partial(kernel, (n_f, n_c, nq, nw)), out_shape=j...  246 us

profile of v4, /device:TPU:29, one launch (start us, length us, event | category | flops | bytes accessed | tf_op | source)
XLA Modules:
  0.0 251.7 jit_solution(15889141022149336288)
XLA Ops:
  0.0 1.0 fusion.2
  1.0 1.0 pad_maximum_fusion
  2.1 246.4 %shard_map.64 = bf16[512,2048]{1,0:T(8,128)(2,1)} custom-call(s32[1,4,8]{2,1,0:T(4,128)} %lists.1, bf16[512,8192]{1,0:T(8,128)(2,1)} %tokens.1, bf16[1024,1024]{1,0:T(8,128)(2,1)} %wq.1, bf16[1024,1024]{1,0:T(8,128)(2,1)} %wo.1, bf16[2,128,1024]{2,1,0:T(8,128)(2,1)} %bitcast.2, bf16[2,128,1024]{2,1,0:T(8,128)(2,1)} %bitcast.3, ...), custom_call_target="tpu_custom_call" | custom-call | tf_op jit(solution)/shard_map/pallas_call | solution.py:471
  248.5 3.2 %copy.8 = bf16[512,2048]{1,0:T(8,128)(2,1)} copy(bf16[512,2048]{1,0:T(8,128)(2,1)} %shard_map.64) | data formatting | bytes 4194304
  (2 shorter events, 0.0 us)
